TPU v7x, 256 devices: a whole 4x4x8 slice. The times are simulated.
256 devices in a mesh: rep: 8 (over x, z_hi), seq: 4 (over y), tp: 8 (over z_lo, core).
Axes of the slice: x: 4, y: 4, z: 8 (z_hi: 2, z_lo: 4; z = z_hi * 4 + z_lo), core: 2. Of those that a mesh axis runs over, the one named last changes fastest.
Arguments:
- hidden_in: bfloat16 [32768, 1536], P(('rep', 'seq', 'tp')), may hold values from -3 to 3
- routes: int32 [32768, 4], P(('rep', 'seq', 'tp')), may hold values from 0 to 31, all different within a row; in each aligned block of 128 rows (0 to 127, 128 to 255, ...) at most 24 rows name the same one
- prefix_len: int32 [8], replicated, may hold values from 256 to 2048, as said below
- cache: bfloat16 [8, 2, 2048, 256], P(None, None, ('rep', 'seq')), may hold values from -400 to 400, as said below
- attn_gain: float32 [1536], replicated, may hold values from 0.1 to 1.9
- w_query: bfloat16 [1536, 1024], P(None, 'tp'), may hold values from -0.375 to 0.375
- w_keyval: bfloat16 [2, 1536, 256], replicated, may hold values from -0.15625 to 0.15625
- w_out: bfloat16 [1024, 1536], P('tp'), may hold values from -0.375 to 0.375
- moe_gain: float32 [1536], replicated, may hold values from 0.1 to 1.9
- w_router: bfloat16 [1536, 32], replicated, may hold values from -0.15625 to 0.15625
- expert_in: bfloat16 [32, 1536, 1536], P(('seq', 'tp')), may hold values from -0.15625 to 0.15625
- expert_out: bfloat16 [32, 768, 1536], P(('seq', 'tp')), may hold values from -0.875 to 0.875
Outputs:
- hidden_out: bfloat16 [32768, 1536], P(('rep', 'seq', 'tp'))
- new_cache: bfloat16 [32768, 512], P(('rep', 'seq'), 'tp')
Inputs may be any that keep to these rules, and one draw needn't show every extreme that they name: `routes`: each row names 4 different experts; within the rows of one device (aligned blocks of 128 rows) no expert is named by more than 24 rows. prefix_len[r] cached positions (0 to prefix_len[r] - 1) of request r are valid; some request has 2048. cache[r, g, p, 0:128] is a key, cache[r, g, p, 128:] a value.
All inputs are finite; a program needn't handle non-finite values.
Results may differ from a plain program's by a relative error of at most 0.029.
The roundings to bfloat16 on the way count: a program that leaves them out, or rounds other values in their place, can miss the bound.
Values may be sent and summed in bfloat16 or wider, within the bound.
No kernel may reach another device: no remote copies, remote signals or barrier semaphores. Data moves between devices by JAX's collectives and lax.ppermute only.
A program may use at most 64 MiB of HBM per device.

v0:
```python
import jax
import jax.numpy as jnp
from jax import lax
from jax.sharding import PartitionSpec as P

CAP = 24
epsilon = 1e-06
masked_score = -1e30


def rms_scale(rows, gain):
    values = rows.astype(jnp.float32)
    inverse = lax.rsqrt(jnp.mean(values * values, axis=-1, keepdims=True) + epsilon)
    return (values * inverse * gain).astype(jnp.bfloat16)


def attend(state, query_rows, block, visible, scale):
    best, total, summed = state
    head_dim = block.shape[1] // 2
    scores = (
        lax.dot_general(
            query_rows,
            block[:, :head_dim],
            (((1,), (1,)), ((), ())),
            preferred_element_type=jnp.float32,
        )
        * scale
    )
    scores = jnp.where(visible, scores, masked_score)
    new_best = jnp.maximum(best, jnp.max(scores, axis=1))
    weights = jnp.where(visible, jnp.exp(scores - new_best[:, None]), 0.0)
    factor = jnp.exp(best - new_best)
    total = total * factor + jnp.sum(weights, axis=1)
    summed = summed * factor[:, None] + jnp.dot(
        weights.astype(jnp.bfloat16), block[:, head_dim:], preferred_element_type=jnp.float32
    )
    return (new_best, total, summed)


def body(
    hidden_in,
    routes,
    prefix_len,
    cache,
    attn_gain,
    w_query,
    w_keyval,
    w_out,
    moe_gain,
    w_router,
    expert_in,
    expert_out,
):
    tp_count = lax.axis_size("tp")
    seq_count = lax.axis_size("seq")
    rep_count = lax.axis_size("rep")
    tp_index = lax.axis_index("tp")
    seq_index = lax.axis_index("seq")
    rep_index = lax.axis_index("rep")
    rows_dev, width = hidden_in.shape
    kv_heads = w_keyval.shape[0]
    pair_cols = w_keyval.shape[2]
    head_dim = pair_cols // 2
    query_cols = w_query.shape[1]
    heads_dev = query_cols // head_dim
    piece_len = rows_dev * tp_count
    scale = 1.0 / float(head_dim) ** 0.5
    kv_index = tp_index // (tp_count // kv_heads)
    normed = rms_scale(hidden_in, attn_gain)
    head_weight = lax.dynamic_index_in_dim(w_keyval, kv_index, 0, keepdims=False)
    joined = jnp.concatenate([w_query, head_weight], axis=1)
    projected = jnp.dot(
        lax.all_gather(normed, "tp", axis=0, tiled=True), joined, preferred_element_type=jnp.float32
    ).astype(jnp.bfloat16)
    count_rows = piece_len * heads_dev
    query_rows = projected[:, :query_cols]
    fresh = projected[:, query_cols:]
    col_width = kv_heads * pair_cols // tp_count
    new_cache = lax.dynamic_slice_in_dim(fresh, tp_index * col_width % pair_cols, col_width, 1)
    own_pages = lax.dynamic_index_in_dim(cache, kv_index, 1, keepdims=True)
    fetched = lax.all_to_all(own_pages, "rep", split_axis=0, concat_axis=2, tiled=True)
    page_rows = fetched.shape[2]
    pages = fetched.reshape(page_rows, pair_cols)
    page_len = page_rows // rep_count
    length = lax.dynamic_index_in_dim(prefix_len, rep_index, 0, keepdims=False)
    row_ids = jnp.arange(page_rows, dtype=jnp.int32)

    def page_visible(source):
        position = (row_ids // page_len * seq_count + source) * page_len + row_ids % page_len
        return (position < length)[None, :]

    def fresh_visible(source, query_piece):
        token = jnp.arange(count_rows, dtype=jnp.int32) // heads_dev + query_piece * piece_len
        key_pos = source * piece_len + jnp.arange(piece_len, dtype=jnp.int32)
        return key_pos[None, :] <= token[:, None]

    start_state = (
        jnp.full((count_rows,), masked_score, jnp.float32),
        jnp.zeros((count_rows,), jnp.float32),
        jnp.zeros((count_rows, head_dim), jnp.float32),
    )
    shard_rows = page_rows + piece_len
    local_keys = jnp.concatenate([pages, fresh], axis=0)

    def fold_shard(state, shard, source):
        state = attend(state, query_rows, shard[:page_rows], page_visible(source), scale)

        def with_fresh(inner):
            return attend(
                inner, query_rows, shard[page_rows:], fresh_visible(source, seq_index), scale
            )

        return lax.cond(source <= seq_index, with_fresh, lambda inner: inner, state)

    state = start_state
    gathered = lax.all_gather(local_keys, "seq", axis=0, tiled=True)
    count = gathered.shape[0] // shard_rows
    shards = gathered.reshape(count, shard_rows, pair_cols)

    def advance(inner, item):
        offset, shard = item
        return (fold_shard(inner, shard, offset), None)

    state, _ = lax.scan(advance, state, (jnp.arange(count, dtype=jnp.int32), shards))
    best, total, summed = state
    attended = (summed / total[:, None]).astype(jnp.bfloat16)
    rows = attended
    head_total = lax.psum_scatter(
        jnp.dot(rows, w_out, preferred_element_type=jnp.float32),
        "tp",
        scatter_dimension=0,
        tiled=True,
    )
    mid = (hidden_in.astype(jnp.float32) + head_total).astype(jnp.bfloat16)
    normed_moe = rms_scale(mid, moe_gain)
    experts_all = w_router.shape[1]
    top = routes.shape[1]
    expert_ids = jnp.arange(experts_all, dtype=jnp.int32)
    logits = jnp.dot(normed_moe, w_router, preferred_element_type=jnp.float32)
    matches = routes[:, :, None] == expert_ids[None, None, :]
    chosen = jnp.sum(jnp.where(matches, logits[:, None, :], 0.0), axis=2)
    raised = jnp.exp(chosen)
    gates = raised / jnp.sum(raised, axis=1, keepdims=True)
    flat_routes = routes.reshape(rows_dev * top)
    onehot = (flat_routes[:, None] == expert_ids[None, :]).astype(jnp.int32)
    before = jnp.cumsum(onehot, axis=0) - onehot
    slot = jnp.sum(before * onehot, axis=1)
    target = flat_routes * CAP + slot
    outgoing = (
        jnp.zeros((experts_all * CAP, width), jnp.bfloat16)
        .at[target]
        .set(jnp.repeat(normed_moe, top, axis=0))
    )
    group_count = seq_count * tp_count
    local_experts = expert_in.shape[0]
    inner_dim = expert_out.shape[1]
    arrived = lax.all_to_all(
        outgoing.reshape(group_count, local_experts, CAP, width),
        ("seq", "tp"),
        split_axis=0,
        concat_axis=0,
        tiled=True,
    )
    rows = arrived[:, 0].reshape(-1, width)
    inner = jnp.dot(rows, expert_in[0], preferred_element_type=jnp.float32)
    active = (jnp.maximum(inner[:, :inner_dim], 0.0) * inner[:, inner_dim:]).astype(jnp.bfloat16)
    output = jnp.dot(active, expert_out[0], preferred_element_type=jnp.float32).astype(jnp.bfloat16)
    results = [output.reshape(arrived.shape[0], arrived.shape[2], width)]
    returned = lax.all_to_all(
        jnp.stack(results, axis=1), ("seq", "tp"), split_axis=0, concat_axis=0, tiled=True
    )
    picked = returned.reshape(experts_all * CAP, width)[target].reshape(rows_dev, top, width)
    mixed = jnp.sum(gates[:, :, None] * picked.astype(jnp.float32), axis=1)
    hidden_out = (mid.astype(jnp.float32) + mixed).astype(jnp.bfloat16)
    return (hidden_out, new_cache)


def solution(mesh):
    placed = (
        P(("rep", "seq", "tp"), None),
        P(("rep", "seq", "tp"), None),
        P(),
        P(None, None, ("rep", "seq"), None),
        P(),
        P(None, "tp"),
        P(),
        P("tp", None),
        P(),
        P(),
        P(("seq", "tp"), None, None),
        P(("seq", "tp"), None, None),
    )
    return jax.shard_map(
        body,
        mesh=mesh,
        in_specs=placed,
        out_specs=(P(("rep", "seq", "tp"), None), P(("rep", "seq"), "tp")),
        check_vma=False,
    )
```

profile of v0, /device:TPU:1, one launch (start us, length us, event | category | flops | bytes accessed | tf_op | source)
XLA Modules:
  0.0 418.8 jit_solution(9488731846069213498)
XLA Ops:
  7.2 1.3 fusion.57
  8.6 1.9 fusion.59
  10.5 1.7 constant_dynamic-slice_fusion.2
  12.2 11.5 %all-to-all-start = ((bf16[8,1,64,256]{3,2,1,0:T(8,128)(2,1)}), bf16[8,1,64,256]{3,2,1,0:T(8,128)(2,1)S(1)}, u32[]{:S(2)}, u32[]{:S(2)}) async-start(bf16[8,1,64,256]{3,2,1,0:T(8,128)(2,1)} %constant_dynamic-slice_fusion.2), calls=%async_computation | async-start | bytes 524288 | tf_op jit(solution)/shard_map/all_to_all | solution.py:81
  23.7 2.1 dynamic-slice_bitcast_fusion.1
  25.8 8.2 %all-to-all-done = bf16[8,1,64,256]{3,2,1,0:T(8,128)(2,1)S(1)} async-done(((bf16[8,1,64,256]{3,2,1,0:T(8,128)(2,1)}), bf16[8,1,64,256]{3,2,1,0:T(8,128)(2,1)S(1)}, u32[]{:S(2)}, u32[]{:S(2)}) %all-to-all-start) | async-done | bytes 262176 | tf_op jit(solution)/shard_map/all_to_all | solution.py:81
  34.2 26.8 %all-gather.3.cloned.1.call-done = bf16[1024,1536]{1,0:T(8,128)(2,1)} async-done(((bf16[128,1536]{1,0:T(8,128)(2,1)}), bf16[1024,1536]{1,0:T(8,128)(2,1)}) %all-gather.3.cloned.1.call-update) | async-done | bytes 3145744 | tf_op jit(solution)/shard_map/all_gather | solution.py:73
  61.0 3.5 convolution_convert_fusion.1
  66.2 1.0 pad_maximum_fusion
  68.1 1.0 slice.75
  69.2 41.3 %all-gather.5.cloned.1.call-done = bf16[6144,256]{0,1:T(8,128)(2,1)} async-done(((bf16[1536,256]{0,1:T(8,128)(2,1)}), bf16[6144,256]{0,1:T(8,128)(2,1)}) %all-gather.5.cloned.1.call-update) | async-done | bytes 3145744 | tf_op jit(solution)/shard_map/all_gather | solution.py:116
  110.6 4.6 %copy.48 = bf16[6144,256]{1,0:T(8,128)(2,1)} copy(bf16[6144,256]{0,1:T(8,128)(2,1)} %all-gather.5.cloned.1.call-done) | data formatting | bytes 6291456
  116.0 39.8 %while.20 = (s32[]{:T(128)}, f32[1024]{0:T(1024)S(1)}, f32[1024]{0:T(1024)S(1)}, f32[1024,128]{1,0:T(8,128)}, s32[4]{0:T(128)S(1)}, /*index=5*/s32[]{:T(128)}, s...) while((s32[]{:T(128)}, f32[1024]{0:T(1024)S(1)}, ...), condition=%wide.region_8.9_spmd.clone.clone, body=%wide.region_1.8_spmd.clone.clone.sunk | while | flops 829438464 | bytes 24546600 | solution.py:124
  117.2 1.3 fusion.91
  118.5 1.0 dynamic-slice_bitcast_fusion.3
  119.5 1.2 constant_dynamic-slice_fusion.4
  121.7 2.7 convolution_add_fusion.2
  124.4 6.2 %conditional.4 = ((f32[1024]{0:T(1024)S(1)}, f32[1024]{0:T(1024)S(1)}, f32[1024,128]{1,0:T(8,128)})) conditional(s32[]{:T(128)} %convert_element_type.129, (f32[1024]{0:T(1024)S(1)}, f32[1024]{0:T(1024)S(1)}, f32[1024,128]{1,0:T(8,128)}) %tuple.70, (s32[]{:T(128)}, s32[]{:T(128)}, bf16[1,1536,256]{2,1,0:T(8,128)(2,1)S(1)}, ...), branch_computations={%region_4.4_spmd, %region_5.7_spmd} | conditional | flops 553914368 | bytes 14516288 | solution.py:113
  125.8 1.5 fusion.10
  127.4 3.3 fusion.13
  131.8 1.3 fusion.91
  133.1 1.0 dynamic-slice_bitcast_fusion.3
  134.1 1.2 constant_dynamic-slice_fusion.4
  136.3 2.7 convolution_add_fusion.2
  140.2 1.3 fusion.91
  141.5 1.0 dynamic-slice_bitcast_fusion.3
  142.5 1.2 constant_dynamic-slice_fusion.4
  144.7 2.7 convolution_add_fusion.2
  148.6 1.3 fusion.91
  149.9 1.0 dynamic-slice_bitcast_fusion.3
  150.9 1.2 constant_dynamic-slice_fusion.4
  153.1 2.7 convolution_add_fusion.2
  155.8 4.8 %fusion.65 = f32[1024,1536]{1,0:T(8,128)} fusion(bf16[128,1536]{1,0:T(8,128)(2,1)} %param.23, f32[1024,128]{1,0:T(8,128)} %get-tuple-element.277, f32[1024]{0:T(1024)S(1)} %get-tuple-element.278), kind=kOutput, calls=%fused_computation.89 | convolution fusion | flops 402915328 | bytes 7213056 | tf_op jit(solution)/shard_map/dot_general | solution.py:129
  162.0 1.2 reduce-window.6
  163.5 87.9 %reduce-scatter.2.cloned.1.call-done = f32[128,1536]{1,0:T(8,128)} async-done(((f32[1024,1536]{1,0:T(8,128)}), f32[128,1536]{1,0:T(8,128)}) %reduce-scatter.2.cloned.1.call-update) | async-done | bytes 786448 | tf_op jit(solution)/shard_map/reduce_scatter | solution.py:128
  251.5 1.3 fusion.61
  253.0 1.6 broadcast_in_dim.96
  254.5 3.7 reshape.208
  258.2 5.5 %scatter_custom_fusion = bf16[768,1536]{1,0:T(8,128)(2,1)} fusion(s32[512]{0:T(512)S(1)} %bitcast.64, bf16[512,1536]{1,0:T(8,128)(2,1)} %reshape.208, bf16[]{:T(256)} %constant.204.clone.1), kind=kCustom, calls=%fused_computation.76 | custom fusion | bytes 2359808 | tf_op jit(solution)/shard_map/scatter | solution.py:152
  263.8 63.9 %all_to_all.19 = bf16[32,1,24,1536]{3,2,1,0:T(8,128)(2,1)S(1)} all-to-all(bf16[32,1,24,1536]{3,2,1,0:T(8,128)(2,1)} %bitcast.60), channel_id=1, replica_groups=mesh['rep'=8,'seq'=4,'tp'=8] {'seq','tp'}, dimensions={0} | all-to-all | bytes 4718592 | tf_op jit(solution)/shard_map/all_to_all | solution.py:157
  327.7 5.7 %fusion.46 = f32[768,1536]{1,0:T(8,128)S(1)} fusion(bf16[768,1536]{1,0:T(8,128)(2,1)S(1)} %bitcast.62, bf16[1,1536,1536]{2,1,0:T(8,128)(2,1)} %param.26), kind=kOutput, calls=%fused_computation.57 | convolution fusion | flops 3623878656 | bytes 11796480 | tf_op jit(solution)/shard_map/dot_general | solution.py:165
  333.4 3.4 convolution_convert_fusion
  336.7 4.7 %all-to-all-start.2 = ((bf16[32,1,24,1536]{3,2,1,0:T(8,128)(2,1)}), bf16[32,1,24,1536]{3,2,1,0:T(8,128)(2,1)}, u32[]{:S(2)}, u32[]{:S(2)}) async-start(bf16[32,1,24,1536]{3,2,1,0:T(8,128)(2,1)} %bitcast.61), calls=%async_computation.3 | async-start | bytes 4718592 | tf_op jit(solution)/shard_map/all_to_all | solution.py:169
  341.5 1.6 constant_dynamic-slice_fusion.1
  343.5 53.2 %all-to-all-done.2 = bf16[32,1,24,1536]{3,2,1,0:T(8,128)(2,1)} async-done(((bf16[32,1,24,1536]{3,2,1,0:T(8,128)(2,1)}), bf16[32,1,24,1536]{3,2,1,0:T(8,128)(2,1)}, u32[]{:S(2)}, u32[]{:S(2)}) %all-to-all-start.2) | async-done | bytes 2359328 | tf_op jit(solution)/shard_map/all_to_all | solution.py:169
  396.7 6.4 %gather_fusion = bf16[512,1536]{1,0:T(8,128)(2,1)} fusion(bf16[768,1536]{1,0:T(8,128)(2,1)} %bitcast.14, s32[1024]{0:T(1024)S(1)} %pad_clamp_fusion), kind=kCustom, calls=%fused_computation | custom fusion | bytes 3147776 | tf_op jit(solution)/shard_map/gather | solution.py:172
  403.1 4.2 %reshape.195 = f32[128,4,1536]{2,1,0:T(4,128)} reshape(bf16[512,1536]{1,0:T(8,128)(2,1)} %gather_fusion) | data formatting | bytes 4718592 | tf_op jit(solution)/shard_map/convert_element_type | solution.py:173
  407.3 4.2 multiply_reduce_fusion
  (90 shorter events, 14.3 us)
Async XLA Ops:
  7.2 326.2 %copy-start = (bf16[1,768,1536]{2,1,0:T(8,128)(2,1)S(1)}, bf16[1,768,1536]{2,1,0:T(8,128)(2,1)}, u32[]{:S(2)}) copy-start(bf16[1,768,1536]{2,1,0:T(8,128)(2,1)} %param.27) | copy-start | bytes 7077892
  7.2 53.8 %copy-start.7 = (bf16[1536,128]{1,0:T(8,128)(2,1)S(1)}, bf16[1536,128]{1,0:T(8,128)(2,1)}, u32[]{:S(2)}) copy-start(bf16[1536,128]{1,0:T(8,128)(2,1)} %param.21) | copy-start | bytes 1179652
  7.2 53.8 %all-gather.3.cloned.1.call-start = ((), (), s32[]{:S(2)}) async-start(), calls=%async_computation.4 | async-start | bytes 3538944 | tf_op jit(solution)/shard_map/all_gather | solution.py:73
  12.2 21.8 %all-to-all-start = ((bf16[8,1,64,256]{3,2,1,0:T(8,128)(2,1)}), bf16[8,1,64,256]{3,2,1,0:T(8,128)(2,1)S(1)}, u32[]{:S(2)}, u32[]{:S(2)}) async-start(bf16[8,1,64,256]{3,2,1,0:T(8,128)(2,1)} %constant_dynamic-slice_fusion.2), calls=%async_computation | async-start | bytes 524288 | tf_op jit(solution)/shard_map/all_to_all | solution.py:81
  23.7 86.9 %all-gather.5.cloned.1.call-start = ((), (), s32[]{:S(2)}) async-start(), calls=%async_computation.5 | async-start | bytes 3932160 | tf_op jit(solution)/shard_map/all_gather | solution.py:116
  64.5 0.9 copy-start.3
  65.4 2.1 copy-start.8
  65.4 0.8 copy-start.2
  67.2 184.3 %reduce-scatter.2.cloned.1.call-start = ((), (), s32[]{:S(2)}) async-start(), calls=%async_computation.6 | async-start | bytes 7077888 | tf_op jit(solution)/shard_map/reduce_scatter | solution.py:128
  160.7 0.7 copy-start.5
  160.7 90.8 %copy-start.1 = (bf16[128,1536]{1,0:T(8,128)(2,1)S(1)}, bf16[128,1536]{1,0:T(8,128)(2,1)}, u32[]{:S(2)}) copy-start(bf16[128,1536]{1,0:T(8,128)(2,1)} %param.16) | copy-start | bytes 1179652
  160.7 92.1 %copy-start.6 = (f32[1536]{0:T(1024)S(1)}, f32[1536]{0:T(1024)}, u32[]{:S(2)}) copy-start(f32[1536]{0:T(1024)} %param.24) | copy-start | bytes 18436
  336.7 6.3 %copy-start.4 = (bf16[1536,32]{0,1:T(8,128)(2,1)S(1)}, bf16[1536,32]{0,1:T(8,128)(2,1)}, u32[]{:S(2)}) copy-start(bf16[1536,32]{0,1:T(8,128)(2,1)} %param.25) | copy-start | bytes 294916
  336.7 60.0 %all-to-all-start.2 = ((bf16[32,1,24,1536]{3,2,1,0:T(8,128)(2,1)}), bf16[32,1,24,1536]{3,2,1,0:T(8,128)(2,1)}, u32[]{:S(2)}, u32[]{:S(2)}) async-start(bf16[32,1,24,1536]{3,2,1,0:T(8,128)(2,1)} %bitcast.61), calls=%async_computation.3 | async-start | bytes 4718592 | tf_op jit(solution)/shard_map/all_to_all | solution.py:169
Sparse Core Ops, SparseCore 0:
  10.6 50.3 all-gather.2
  67.3 43.2 all-gather.4
  160.8 90.5 reduce-scatter.1
where the time goes:
time: 421 us; the launch traced here: 419 us
  waiting for transfers between devices  218 us (52%)
  blocking collectives  63.9 us (15%)
  local copies, waits for them, and re-layouts  48.4 us (11%)
  matrix products  34.3 us (8%)
  other arithmetic  21.2 us (5%)
  starting transfers between devices  16.5 us (4%)
  between operations  14 us (3%)
    reduce_scatter x1, waiting for transfers between devices, body(): lax.psum_scatter(jnp.dot(rows, w_out, preferred_element_type=jnp.float32)...  87.9 us
    all_to_all x1, blocking collectives, body(): lax.all_to_all(outgoing.reshape(group_count, local_experts, CAP, width),...  63.9 us
    all_to_all x1, waiting for transfers between devices, body(): lax.all_to_all(jnp.stack(results, axis=1), ('seq', 'tp'), split_axis=0, c...  53.2 us
    all_gather x1, waiting for transfers between devices, body(): gathered = lax.all_gather(local_keys, 'seq', axis=0, tiled=True)  41.3 us
    all_gather x1, waiting for transfers between devices, body(): lax.all_gather(normed, 'tp', axis=0, tiled=True)  26.8 us
    dot_general x5, matrix products, attend(): jnp.dot(weights.astype(jnp.bfloat16), block[:, head_dim:], preferred_elem...  14.1 us
    all_to_all x1, starting transfers between devices, body(): lax.all_to_all(own_pages, 'rep', split_axis=0, concat_axis=2, tiled=True)  11.5 us
  transfers between devices with their start and end apart: 5, of which 5 were waited for; matrix products, arithmetic and copies ran while one was open for 2% of the time, Pallas kernels for 0%

commit v1 on v0

--- a/solution.py
+++ b/solution.py
@@ -70,7 +70,11 @@
     head_weight = lax.dynamic_index_in_dim(w_keyval, kv_index, 0, keepdims=False)
     joined = jnp.concatenate([w_query, head_weight], axis=1)
     projected = jnp.dot(
-        lax.all_gather(normed, "tp", axis=0, tiled=True), joined, preferred_element_type=jnp.float32
+        jnp.concatenate(
+            lax.all_to_all(jnp.stack([normed] * lax.axis_size("tp")), "tp", 0, 0), axis=0
+        ),
+        joined,
+        preferred_element_type=jnp.float32,
     ).astype(jnp.bfloat16)
     count_rows = piece_len * heads_dev
     query_rows = projected[:, :query_cols]

time: 421 us -> 464 us (1.10)
  waiting for transfers between devices: 218 us -> 254 us
  starting transfers between devices: 16.5 us -> 23.9 us
    all_to_all x0 -> x1, waiting for transfers between devices: none -> 68.4 us  [body(): lax.all_to_all(jnp.stack([normed] * lax.axis_size('tp')), 'tp', 0, 0)]
    all_gather x1 -> x0, waiting for transfers between devices: 26.8 us -> none  [body(): lax.all_gather(normed, 'tp', axis=0, tiled=True)]
    all_to_all x0 -> x1, starting transfers between devices: none -> 7.52 us  [body(): lax.all_to_all(jnp.stack([normed] * lax.axis_size('tp')), 'tp', 0, 0)]
    all_gather x1, waiting for transfers between devices: 41.3 us -> 36.6 us  [body(): gathered = lax.all_gather(local_keys, 'seq', axis=0, tiled=True)]
where the time goes in v1:
time: 464 us; the launch traced here: 463 us
  waiting for transfers between devices  254 us (55%)
  blocking collectives  63.9 us (14%)
  local copies, waits for them, and re-layouts  48.7 us (10%)
  matrix products  34.4 us (7%)
  starting transfers between devices  23.9 us (5%)
  other arithmetic  20.2 us (4%)
  between operations  14.2 us (3%)
    reduce_scatter x1, waiting for transfers between devices, body(): lax.psum_scatter(jnp.dot(rows, w_out, preferred_element_type=jnp.float32)...  87.9 us
    all_to_all x1, waiting for transfers between devices, body(): lax.all_to_all(jnp.stack([normed] * lax.axis_size('tp')), 'tp', 0, 0)  68.4 us
    all_to_all x1, blocking collectives, body(): lax.all_to_all(outgoing.reshape(group_count, local_experts, CAP, width),...  63.9 us
    all_to_all x1, waiting for transfers between devices, body(): lax.all_to_all(jnp.stack(results, axis=1), ('seq', 'tp'), split_axis=0, c...  53.2 us
    all_gather x1, waiting for transfers between devices, body(): gathered = lax.all_gather(local_keys, 'seq', axis=0, tiled=True)  36.6 us
    dot_general x5, matrix products, attend(): jnp.dot(weights.astype(jnp.bfloat16), block[:, head_dim:], preferred_elem...  14.1 us
    all_to_all x1, starting transfers between devices, body(): lax.all_to_all(own_pages, 'rep', split_axis=0, concat_axis=2, tiled=True)  11.5 us
  transfers between devices with their start and end apart: 5, of which 5 were waited for; matrix products, arithmetic and copies ran while one was open for 2% of the time, Pallas kernels for 0%

profile of v1, /device:TPU:1, one launch (start us, length us, event | category | flops | bytes accessed | tf_op | source)
XLA Modules:
  0.0 462.5 jit_solution(16618523831992030490)
XLA Ops:
  7.2 1.8 constant_dynamic-slice_fusion.2
  9.0 11.5 %all-to-all-start = ((bf16[8,1,64,256]{3,2,1,0:T(8,128)(2,1)}), bf16[8,1,64,256]{3,2,1,0:T(8,128)(2,1)S(1)}, u32[]{:S(2)}, u32[]{:S(2)}) async-start(bf16[8,1,64,256]{3,2,1,0:T(8,128)(2,1)} %constant_dynamic-slice_fusion.2), calls=%async_computation | async-start | bytes 524288 | tf_op jit(solution)/shard_map/all_to_all | solution.py:85
  20.5 1.2 fusion.57
  21.7 1.2 fusion.59
  22.8 7.8 %all-to-all-done = bf16[8,1,64,256]{3,2,1,0:T(8,128)(2,1)S(1)} async-done(((bf16[8,1,64,256]{3,2,1,0:T(8,128)(2,1)}), bf16[8,1,64,256]{3,2,1,0:T(8,128)(2,1)S(1)}, u32[]{:S(2)}, u32[]{:S(2)}) %all-to-all-start) | async-done | bytes 262176 | tf_op jit(solution)/shard_map/all_to_all | solution.py:85
  30.7 2.0 stack.2
  32.6 7.5 %all-to-all-start.1 = ((bf16[8,128,1536]{2,1,0:T(8,128)(2,1)}), bf16[8,128,1536]{2,1,0:T(8,128)(2,1)}, u32[]{:S(2)}, u32[]{:S(2)}) async-start(bf16[8,128,1536]{2,1,0:T(8,128)(2,1)} %stack.2), calls=%async_computation.1 | async-start | bytes 6291456 | tf_op jit(solution)/shard_map/all_to_all | solution.py:74
  40.2 2.1 dynamic-slice_bitcast_fusion.1
  42.4 68.4 %all-to-all-done.1 = bf16[8,128,1536]{2,1,0:T(8,128)(2,1)} async-done(((bf16[8,128,1536]{2,1,0:T(8,128)(2,1)}), bf16[8,128,1536]{2,1,0:T(8,128)(2,1)}, u32[]{:S(2)}, u32[]{:S(2)}) %all-to-all-start.1) | async-done | bytes 3145760 | tf_op jit(solution)/shard_map/all_to_all | solution.py:74
  110.8 3.6 convolution_convert_fusion.1
  117.3 36.6 %all-gather.2.cloned.1.call-done = bf16[6144,256]{0,1:T(8,128)(2,1)} async-done(((bf16[1536,256]{0,1:T(8,128)(2,1)}), bf16[6144,256]{0,1:T(8,128)(2,1)}) %all-gather.2.cloned.1.call-update) | async-done | bytes 3145744 | tf_op jit(solution)/shard_map/all_gather | solution.py:120
  153.9 4.6 %copy.48 = bf16[6144,256]{1,0:T(8,128)(2,1)} copy(bf16[6144,256]{0,1:T(8,128)(2,1)} %all-gather.2.cloned.1.call-done) | data formatting | bytes 6291456
  159.4 39.8 %while.20 = (s32[]{:T(128)}, f32[1024]{0:T(1024)S(1)}, f32[1024]{0:T(1024)S(1)}, f32[1024,128]{1,0:T(8,128)}, s32[4]{0:T(128)S(1)}, /*index=5*/s32[]{:T(128)}, s...) while((s32[]{:T(128)}, f32[1024]{0:T(1024)S(1)}, ...), condition=%wide.region_8.9_spmd.clone.clone, body=%wide.region_1.8_spmd.clone.clone.sunk | while | flops 829438464 | bytes 24546600 | solution.py:128
  160.6 1.3 fusion.91
  161.9 1.0 dynamic-slice_bitcast_fusion.3
  162.8 1.2 constant_dynamic-slice_fusion.4
  165.1 2.7 convolution_add_fusion.2
  167.8 6.2 %conditional.4 = ((f32[1024]{0:T(1024)S(1)}, f32[1024]{0:T(1024)S(1)}, f32[1024,128]{1,0:T(8,128)})) conditional(s32[]{:T(128)} %convert_element_type.129, (f32[1024]{0:T(1024)S(1)}, f32[1024]{0:T(1024)S(1)}, f32[1024,128]{1,0:T(8,128)}) %tuple.70, (s32[]{:T(128)}, s32[]{:T(128)}, bf16[1,1536,256]{2,1,0:T(8,128)(2,1)S(1)}, ...), branch_computations={%region_4.4_spmd, %region_5.7_spmd} | conditional | flops 553914368 | bytes 14516288 | solution.py:117
  169.2 1.5 fusion.10
  170.7 3.3 fusion.13
  175.2 1.3 fusion.91
  176.5 1.0 dynamic-slice_bitcast_fusion.3
  177.4 1.2 constant_dynamic-slice_fusion.4
  179.7 2.7 convolution_add_fusion.2
  183.6 1.3 fusion.91
  184.9 1.0 dynamic-slice_bitcast_fusion.3
  185.8 1.2 constant_dynamic-slice_fusion.4
  188.1 2.7 convolution_add_fusion.2
  192.0 1.3 fusion.91
  193.3 1.0 dynamic-slice_bitcast_fusion.3
  194.2 1.2 constant_dynamic-slice_fusion.4
  196.5 2.7 convolution_add_fusion.2
  199.2 4.8 %fusion.65 = f32[1024,1536]{1,0:T(8,128)} fusion(bf16[128,1536]{1,0:T(8,128)(2,1)} %param.23, f32[1024,128]{1,0:T(8,128)} %get-tuple-element.277, f32[1024]{0:T(1024)S(1)} %get-tuple-element.278), kind=kOutput, calls=%fused_computation.89 | convolution fusion | flops 402915328 | bytes 7213056 | tf_op jit(solution)/shard_map/dot_general | solution.py:133
  205.3 1.2 reduce-window.6
  206.9 87.9 %reduce-scatter.2.cloned.1.call-done = f32[128,1536]{1,0:T(8,128)} async-done(((f32[1024,1536]{1,0:T(8,128)}), f32[128,1536]{1,0:T(8,128)}) %reduce-scatter.2.cloned.1.call-update) | async-done | bytes 786448 | tf_op jit(solution)/shard_map/reduce_scatter | solution.py:132
  294.8 1.3 fusion.61
  296.3 1.6 broadcast_in_dim.96
  297.9 3.7 reshape.214
  301.6 5.5 %scatter_custom_fusion = bf16[768,1536]{1,0:T(8,128)(2,1)} fusion(s32[512]{0:T(512)S(1)} %bitcast.65, bf16[512,1536]{1,0:T(8,128)(2,1)} %reshape.214, bf16[]{:T(256)} %constant.204.clone.1), kind=kCustom, calls=%fused_computation.76 | custom fusion | bytes 2359808 | tf_op jit(solution)/shard_map/scatter | solution.py:156
  307.1 63.9 %all_to_all.24 = bf16[32,1,24,1536]{3,2,1,0:T(8,128)(2,1)S(1)} all-to-all(bf16[32,1,24,1536]{3,2,1,0:T(8,128)(2,1)} %bitcast.61), channel_id=1, replica_groups=mesh['rep'=8,'seq'=4,'tp'=8] {'seq','tp'}, dimensions={0} | all-to-all | bytes 4718592 | tf_op jit(solution)/shard_map/all_to_all | solution.py:161
  371.0 5.7 %fusion.46 = f32[768,1536]{1,0:T(8,128)S(1)} fusion(bf16[768,1536]{1,0:T(8,128)(2,1)S(1)} %bitcast.63, bf16[1,1536,1536]{2,1,0:T(8,128)(2,1)} %param.26), kind=kOutput, calls=%fused_computation.57 | convolution fusion | flops 3623878656 | bytes 11796480 | tf_op jit(solution)/shard_map/dot_general | solution.py:169
  376.7 3.4 convolution_convert_fusion
  380.1 4.7 %all-to-all-start.3 = ((bf16[32,1,24,1536]{3,2,1,0:T(8,128)(2,1)}), bf16[32,1,24,1536]{3,2,1,0:T(8,128)(2,1)}, u32[]{:S(2)}, u32[]{:S(2)}) async-start(bf16[32,1,24,1536]{3,2,1,0:T(8,128)(2,1)} %bitcast.62), calls=%async_computation.4 | async-start | bytes 4718592 | tf_op jit(solution)/shard_map/all_to_all | solution.py:173
  384.9 1.6 constant_dynamic-slice_fusion.1
  386.8 53.2 %all-to-all-done.3 = bf16[32,1,24,1536]{3,2,1,0:T(8,128)(2,1)} async-done(((bf16[32,1,24,1536]{3,2,1,0:T(8,128)(2,1)}), bf16[32,1,24,1536]{3,2,1,0:T(8,128)(2,1)}, u32[]{:S(2)}, u32[]{:S(2)}) %all-to-all-start.3) | async-done | bytes 2359328 | tf_op jit(solution)/shard_map/all_to_all | solution.py:173
  440.1 6.4 %gather_fusion = bf16[512,1536]{1,0:T(8,128)(2,1)} fusion(bf16[768,1536]{1,0:T(8,128)(2,1)} %bitcast.15, s32[1024]{0:T(1024)S(1)} %pad_clamp_fusion), kind=kCustom, calls=%fused_computation | custom fusion | bytes 3147776 | tf_op jit(solution)/shard_map/gather | solution.py:176
  446.5 4.2 reshape.201
  450.6 4.2 multiply_reduce_fusion
  (86 shorter events, 14.3 us)
Async XLA Ops:
  7.2 369.5 %copy-start = (bf16[1,768,1536]{2,1,0:T(8,128)(2,1)S(1)}, bf16[1,768,1536]{2,1,0:T(8,128)(2,1)}, u32[]{:S(2)}) copy-start(bf16[1,768,1536]{2,1,0:T(8,128)(2,1)} %param.27) | copy-start | bytes 7077892
  9.0 21.6 %all-to-all-start = ((bf16[8,1,64,256]{3,2,1,0:T(8,128)(2,1)}), bf16[8,1,64,256]{3,2,1,0:T(8,128)(2,1)S(1)}, u32[]{:S(2)}, u32[]{:S(2)}) async-start(bf16[8,1,64,256]{3,2,1,0:T(8,128)(2,1)} %constant_dynamic-slice_fusion.2), calls=%async_computation | async-start | bytes 524288 | tf_op jit(solution)/shard_map/all_to_all | solution.py:85
  32.6 78.2 %all-to-all-start.1 = ((bf16[8,128,1536]{2,1,0:T(8,128)(2,1)}), bf16[8,128,1536]{2,1,0:T(8,128)(2,1)}, u32[]{:S(2)}, u32[]{:S(2)}) async-start(bf16[8,128,1536]{2,1,0:T(8,128)(2,1)} %stack.2), calls=%async_computation.1 | async-start | bytes 6291456 | tf_op jit(solution)/shard_map/all_to_all | solution.py:74
  40.2 113.8 %all-gather.2.cloned.1.call-start = ((), (), s32[]{:S(2)}) async-start(), calls=%async_computation.5 | async-start | bytes 3932160 | tf_op jit(solution)/shard_map/all_gather | solution.py:120
  114.4 2.0 copy-start.6
  114.5 0.8 copy-start.2
  116.2 178.6 %reduce-scatter.2.cloned.1.call-start = ((), (), s32[]{:S(2)}) async-start(), calls=%async_computation.6 | async-start | bytes 7077888 | tf_op jit(solution)/shard_map/reduce_scatter | solution.py:132
  204.1 0.7 copy-start.4
  204.1 90.8 %copy-start.1 = (bf16[128,1536]{1,0:T(8,128)(2,1)S(1)}, bf16[128,1536]{1,0:T(8,128)(2,1)}, u32[]{:S(2)}) copy-start(bf16[128,1536]{1,0:T(8,128)(2,1)} %param.16) | copy-start | bytes 1179652
  204.1 92.1 %copy-start.5 = (f32[1536]{0:T(1024)S(1)}, f32[1536]{0:T(1024)}, u32[]{:S(2)}) copy-start(f32[1536]{0:T(1024)} %param.24) | copy-start | bytes 18436
  380.1 6.3 %copy-start.3 = (bf16[1536,32]{0,1:T(8,128)(2,1)S(1)}, bf16[1536,32]{0,1:T(8,128)(2,1)}, u32[]{:S(2)}) copy-start(bf16[1536,32]{0,1:T(8,128)(2,1)} %param.25) | copy-start | bytes 294916
  380.1 60.0 %all-to-all-start.3 = ((bf16[32,1,24,1536]{3,2,1,0:T(8,128)(2,1)}), bf16[32,1,24,1536]{3,2,1,0:T(8,128)(2,1)}, u32[]{:S(2)}, u32[]{:S(2)}) async-start(bf16[32,1,24,1536]{3,2,1,0:T(8,128)(2,1)} %bitcast.62), calls=%async_computation.4 | async-start | bytes 4718592 | tf_op jit(solution)/shard_map/all_to_all | solution.py:173
Sparse Core Ops, SparseCore 0:
  116.3 37.5 all-gather.1
  204.2 90.5 reduce-scatter.1
